TPU v7x, 32 devices: a whole 2x2x4 slice. The times are simulated.
32 devices in a mesh: freq: 4 (over x, core), tile: 8 (over z, y).
Axes of the slice: x: 2, y: 2, z: 4, core: 2. Of those that a mesh axis runs over, the one named last changes fastest.
Arguments:
- plus_time: bfloat16 [128, 128, 12288], P('freq', None, 'tile'), may hold values from -6 to 6
- minus_time: bfloat16 [128, 128, 12288], P('freq', None, 'tile'), may hold values from -6 to 6
- gate_starts: int32 [128, 48], P('freq', 'tile'), may hold values from 0 to 64
- tile_ranks: int32 [4, 48, 48], P('freq', None, 'tile'), may hold values from 1 to 64, as said below
- u_factors: bfloat16 [4, 48, 48, 2, 64, 256], P('freq', 'tile'), may hold values from -0.109375 to 0.109375
- v_factors: bfloat16 [4, 48, 48, 2, 64, 256], P('freq', None, 'tile'), may hold values from -0.375 to 0.375
Outputs:
- minus_new: bfloat16 [4, 2, 128, 12288], P('freq', None, None, 'tile')
- plus_new: bfloat16 [4, 2, 128, 12288], P('freq', None, None, 'tile')
- cross_gram: float32 [4, 2, 128, 128], P('freq', None, 'tile')
- normal_gram: float32 [4, 2, 128, 128], P('freq', None, 'tile')
Inputs may be any that keep to these rules, and one draw needn't show every extreme that they name: `tile_ranks`: tiles with |i - j| <= 1 have rank 64; every other tile has rank at most 32, and some tile of every draw has exactly 32.
All inputs are finite; a program needn't handle non-finite values.
Results may differ from a plain program's by a relative error of at most 0.014.
Values may be sent and summed in bfloat16 or wider, within the bound.
A program may use at most 192 MiB of HBM per device.

v0:
```python
import math
import jax
import jax.numpy as jnp
from jax import lax
from jax.sharding import PartitionSpec as P

R = 12288
GATE = 64


def extended(x, sides, width):
    for axis, dim in sides:
        size, length = (lax.axis_size(axis), x.shape[dim])
        up = [(i, (i + 1) % size) for i in range(size - 1)]
        down = [(j, i) for i, j in up]
        last = lax.slice_in_dim(x, length - width, length, axis=dim)
        leading = lax.slice_in_dim(x, 0, width, axis=dim)
        before = lax.ppermute(last, axis, up)
        after = lax.ppermute(leading, axis, down)
        x = jnp.concatenate([before, x, after], axis=dim)
    return x


def make_table(freq_count, sample_count):
    freq_ids = lax.broadcasted_iota(jnp.int32, (freq_count, sample_count), 0)
    sample_ids = lax.broadcasted_iota(jnp.int32, (freq_count, sample_count), 1)
    phase_ids = freq_ids * sample_ids % sample_count
    angles = phase_ids.astype(jnp.float32) * (2.0 * math.pi / sample_count)
    amplitude = 1.0 / math.sqrt(GATE)
    return jnp.stack([jnp.cos(angles) * amplitude, -jnp.sin(angles) * amplitude]).astype(
        jnp.bfloat16
    )


def half_signs(entry_count):
    entry_ids = lax.broadcasted_iota(jnp.int32, (entry_count,), 0)
    return jnp.where(entry_ids < entry_count // 2, 1.0, -1.0).astype(jnp.float32)


def gate_field(traces, gate_starts):
    sources, samples, receivers = traces.shape
    blocks = gate_starts.shape[1]
    shaped = traces.reshape(sources, samples, blocks, receivers // blocks)
    sample_ids = lax.broadcasted_iota(jnp.int32, (1, samples, 1, 1), 1)
    starts = gate_starts[:, None, :, None]
    inside = (sample_ids >= starts) & (sample_ids < starts + GATE)
    kept = jnp.where(inside, shaped, jnp.zeros((), traces.dtype))
    return kept.reshape(sources, samples, receivers)


def on_device(plus_time, minus_time, gate_starts, tile_ranks, u_factors, v_factors):
    f_local = u_factors.shape[0]
    row_tiles = u_factors.shape[1]
    all_tiles = u_factors.shape[2]
    col_tiles = v_factors.shape[2]
    rank_depth = v_factors.shape[4]
    half_depth = rank_depth // 2
    freq_total = f_local * lax.axis_size("freq")
    sample_count = plus_time.shape[1]
    stacked = jnp.stack([gate_field(plus_time, gate_starts), gate_field(minus_time, gate_starts)])
    dft_table = make_table(freq_total, sample_count)
    local_spec = jnp.einsum(
        "cft,qstr->fcqsr", dft_table, stacked, preferred_element_type=jnp.float32
    ).astype(jnp.bfloat16)
    spectra = lax.all_to_all(local_spec, "freq", split_axis=0, concat_axis=3, tiled=True)
    both_sources = 2 * spectra.shape[3]
    columns = spectra.reshape(f_local, 2, both_sources, col_tiles, spectra.shape[4] // col_tiles)
    sign_vec = half_signs(both_sources)
    partial_c = jnp.einsum(
        "fijckr,fdsjr->fijcdks", v_factors, columns, preferred_element_type=jnp.float32
    )
    coeff_real = partial_c[:, :, :, 0, 0] - sign_vec * partial_c[:, :, :, 1, 1]
    coeff_imag = partial_c[:, :, :, 0, 1] + sign_vec * partial_c[:, :, :, 1, 0]
    rank_ids = lax.broadcasted_iota(jnp.int32, (1, 1, 1, rank_depth), 3)
    rank_mask = (rank_ids < tile_ranks[:, :, :, None]).astype(jnp.float32)[..., None]
    coeff_all = jnp.stack([coeff_real * rank_mask, coeff_imag * rank_mask], 3).astype(jnp.bfloat16)
    lower_part = coeff_all[:, :, :, :, :half_depth]
    lower_rows = lax.all_to_all(lower_part, "tile", split_axis=1, concat_axis=2, tiled=True)
    products = jnp.einsum(
        "fijckr,fijeks->fcesir",
        u_factors[:, :, :, :, :half_depth],
        lower_rows,
        preferred_element_type=jnp.float32,
    )
    block_start = lax.axis_index("tile") * col_tiles
    local_ids = lax.broadcasted_iota(jnp.int32, (col_tiles,), 0)
    global_cols = block_start + local_ids
    band_list = []
    for offset in (-1, 0, 1):
        band_rows = global_cols + offset
        valid = (band_rows >= 0) & (band_rows < all_tiles)
        clipped = jnp.clip(band_rows, 0, all_tiles - 1)
        picked = coeff_all[:, clipped, local_ids][:, :, :, half_depth:]
        band_list.append(
            jnp.where(valid[None, :, None, None, None], picked, jnp.zeros((), picked.dtype))
        )
    band_upper = jnp.stack(band_list, 1)
    padded_band = extended(band_upper, (("tile", 2),), 1)
    row_global = lax.axis_index("tile") * row_tiles + lax.broadcasted_iota(
        jnp.int32, (row_tiles,), 0
    )
    row_local = lax.broadcasted_iota(jnp.int32, (row_tiles,), 0)
    coeff_band = []
    u_band = []
    for position, offset in enumerate((-1, 0, 1)):
        coeff_band.append(padded_band[:, position, 1 - offset : 1 - offset + row_tiles])
        partner = jnp.clip(row_global - offset, 0, all_tiles - 1)
        u_band.append(u_factors[:, row_local, partner][:, :, :, half_depth:])
    band_products = jnp.einsum(
        "fdickr,fdieks->fcesir",
        jnp.stack(u_band, 1),
        jnp.stack(coeff_band, 1),
        preferred_element_type=jnp.float32,
    )
    products = products + band_products
    resp_real = products[:, 0, 0] - sign_vec[:, None, None] * products[:, 1, 1]
    resp_imag = products[:, 0, 1] + sign_vec[:, None, None] * products[:, 1, 0]
    response = jnp.stack([resp_real, resp_imag], 1).reshape(f_local, 2, both_sources, -1)
    rounded = response.astype(jnp.bfloat16)
    half_count = both_sources // 2
    minus_new = rounded[:, :, :half_count]
    plus_new = rounded[:, :, half_count:]
    gram_parts = jnp.einsum(
        "fczr,fesr->fczes", rounded, plus_new, preferred_element_type=jnp.float32
    )
    gram_real = gram_parts[:, 0, :, 0] + gram_parts[:, 1, :, 1]
    gram_imag = gram_parts[:, 1, :, 0] - gram_parts[:, 0, :, 1]
    row_ids = lax.broadcasted_iota(jnp.int32, (both_sources, 1), 0)
    row_scale = jnp.where(row_ids < half_count, 1.0 / math.sqrt(R), 1.0 / R).astype(jnp.float32)
    gram_all = jnp.stack([gram_real * row_scale, gram_imag * row_scale], 1)
    gram_all = gram_all.reshape(f_local, 2, 2, half_count, half_count).transpose(0, 2, 1, 3, 4)
    gram_total = lax.psum(gram_all.astype(jnp.bfloat16), "tile").astype(jnp.float32)
    row_share = half_count // lax.axis_size("tile")
    own_rows = lax.dynamic_slice_in_dim(
        gram_total, lax.axis_index("tile") * row_share, row_share, 3
    )
    return (minus_new, plus_new, own_rows[:, 0], own_rows[:, 1])


def solution(mesh):
    placed = (
        P("freq", None, "tile"),
        P("freq", None, "tile"),
        P("freq", "tile"),
        P("freq", None, "tile"),
        P("freq", "tile", None, None, None, None),
        P("freq", None, "tile", None, None, None),
    )
    return jax.shard_map(
        on_device,
        mesh=mesh,
        in_specs=placed,
        out_specs=(
            P("freq", None, None, "tile"),
            P("freq", None, None, "tile"),
            P("freq", None, "tile", None),
            P("freq", None, "tile", None),
        ),
        check_vma=False,
    )
```

profile of v0, /device:TPU:0, one launch (start us, length us, event | category | flops | bytes accessed | tf_op | source)
XLA Modules:
  0.0 496.3 jit_solution(5784172588843423811)
XLA Ops:
  7.2 0.7 broadcast_add_fusion
  7.9 0.8 copy.66
  8.6 0.1 multiply_convert_fusion.2
  8.7 0.1 copy.67
  8.8 0.1 fusion.50
  8.9 4.3 broadcast_in_dim.81
  13.2 14.4 %copy.68 = pred[32,128,1536]{2,1,0:T(8,128)(4,1)} copy(pred[32,128,1536]{1,2,0:T(8,128)(4,1)} %bitcast.187) | data formatting | bytes 12582912 | tf_op jit(solution)/shard_map/jit(_where)/broadcast_in_dim | solution.py:47
  27.6 15.3 %select_bitcast_fusion.1 = (bf16[1,32,128,1536]{3,2,1,0:T(8,128)(2,1)S(1)}, bf16[1,32,128,1536]{3,2,1,0:T(8,128)(2,1)}) fusion(pred[32,128,1536]{2,1,0:T(8,128)(4,1)} %copy.68, bf16[32,128,1536]{2,1,0:T(8,128)(2,1)} %param.6, bf16[32,128,1536]{2,1,0:T(8,128)(2,1)} %param.7), kind=kLoop, calls=%fused_computation.27 | loop fusion | flops 12582912 | bytes 56623104 | tf_op jit(solution)/shard_map/jit(_where)/select_n | solution.py:47
  42.9 6.8 %fusion.18 = bf16[4,2,2,32,1536]{4,0,1,3,2:T(4,128)(2,1)S(1)} fusion(bf16[1,32,128,1536]{3,2,1,0:T(8,128)(2,1)} %get-tuple-element.11, bf16[1,32,128,1536]{3,2,1,0:T(8,128)(2,1)S(1)} %get-tuple-element.10, bf16[1,4,128]{2,1,0:T(4,128)(2,1)S(1)} %get-tuple-element.24, bf16[1,4,128]{2,1,0:T(4,128)(2,1)S(1)} %get-tuple-element.25), kind=kOutput, calls=%fused_computation.37 | convolution fusion | flops 252448768 | bytes 26740736 | tf_op jit(solution)/shard_map/cft,qstr->fcqsr/dot_general | solution.py:62
  49.7 0.0 copy-start.3
  49.8 2.4 copy.70
  52.1 4.2 all-to-all-start
  56.4 0.0 copy-done.3
  56.4 0.1 fusion.49
  56.5 19.9 %all-to-all-done = bf16[4,2,2,32,1536]{4,1,3,2,0:T(2,128)(2,1)S(1)} async-done(((bf16[4,2,2,32,1536]{4,1,3,2,0:T(2,128)(2,1)}), bf16[4,2,2,32,1536]{4,1,3,2,0:T(2,128)(2,1)S(1)}, u32[]{:S(2)}, u32[]{:S(2)}) %all-to-all-start) | async-done | bytes 1572896 | tf_op jit(solution)/shard_map/all_to_all | solution.py:65
  76.4 1.4 copy.71
  77.8 3.3 reshape.598
  81.1 32.4 %convolution_bitcast_fusion = f32[1,48,6,2,2,64,256]{6,5,3,1,4,2,0:T(8,128)} fusion(bf16[2,256,6,256,1,1]{3,2,1,0,5,4:T(8,128)(2,1)S(1)} %bitcast.189, bf16[1,48,6,2,64,256]{5,4,3,2,1,0:T(8,128)(2,1)} %param.11), kind=kOutput, calls=%fused_computation.6 | convolution fusion | flops 9663676416 | bytes 95944704 | tf_op jit(solution)/shard_map/fijckr,fdsjr->fijcdks/dot_general | solution.py:69
  113.5 24.0 %fusion.12 = (bf16[1,48,6,1,64,256]{5,4,1,2,3,0:T(8,128)(2,1)S(1)}, bf16[1,48,6,1,64,256]{5,4,1,2,3,0:T(8,128)(2,1)S(1)}) fusion(f32[1,48,6,2,2,64,256]{6,5,3,1,4,2,0:T(8,128)} %convolution_bitcast_fusion, f32[48,6,64]{2,0,1:T(8,128)S(1)} %fusion.49, f32[256]{0:T(256)S(1)} %compare_select_fusion.4), kind=kLoop, calls=%fused_computation.29 | loop fusion | flops 37748736 | bytes 94446592 | tf_op jit(solution)/shard_map/stack | solution.py:76
  137.6 0.0 copy-start
  137.6 0.0 copy-start.1
  137.6 3.6 copy-done
  141.2 2.7 copy-done.1
  143.9 4.1 fusion.13
  148.0 9.0 %copy.77 = bf16[1,48,6,2,32,256]{5,4,2,3,0,1:T(8,128)(2,1)} copy(bf16[1,48,6,2,32,256]{5,4,1,2,3,0:T(8,128)(2,1)} %fusion.13) | data formatting | bytes 18874368 | tf_op jit(solution)/shard_map/slice | solution.py:77
  157.0 6.6 %all-to-all-start.1 = ((bf16[1,48,6,2,32,256]{5,4,2,3,0,1:T(8,128)(2,1)}), bf16[1,48,6,2,32,256]{5,4,2,3,0,1:T(8,128)(2,1)}, u32[]{:S(2)}, u32[]{:S(2)}) async-start(bf16[1,48,6,2,32,256]{5,4,2,3,0,1:T(8,128)(2,1)} %copy.77), calls=%async_computation.1 | async-start | bytes 18874368 | tf_op jit(solution)/shard_map/all_to_all | solution.py:78
  163.6 0.0 all-reduce.2.cloned.1.call-start
  163.7 6.9 %gather_fusion.5 = bf16[6,2,64,256]{3,2,1,0:T(8,128)(2,1)S(1)} fusion(bf16[6,48,2,64,256]{4,3,2,1,0:T(8,128)(2,1)} %bitcast.205, s32[6]{0:T(128)S(1)} %get-tuple-element.28), kind=kCustom, calls=%fused_computation.5 | custom fusion | bytes 786480 | tf_op jit(solution)/shard_map/gather | solution.py:108
  170.7 6.9 %gather_fusion.4 = bf16[6,2,64,256]{3,2,1,0:T(8,128)(2,1)S(1)} fusion(bf16[6,48,2,64,256]{4,3,2,1,0:T(8,128)(2,1)} %bitcast.206, s32[6]{0:T(128)S(1)} %get-tuple-element.29), kind=kCustom, calls=%fused_computation.4 | custom fusion | bytes 786480 | tf_op jit(solution)/shard_map/gather | solution.py:108
  177.6 6.9 %gather_fusion.3 = bf16[6,2,64,256]{3,2,1,0:T(8,128)(2,1)S(1)} fusion(bf16[6,48,2,64,256]{4,3,2,1,0:T(8,128)(2,1)} %bitcast.207, s32[6]{0:T(128)S(1)} %get-tuple-element.30), kind=kCustom, calls=%fused_computation.3 | custom fusion | bytes 786480 | tf_op jit(solution)/shard_map/gather | solution.py:108
  184.7 16.5 %fusion.1 = bf16[48,6,2,64,256]{4,3,0,1,2:T(8,128)(2,1)} fusion(bf16[1,48,6,1,64,256]{5,4,1,2,3,0:T(8,128)(2,1)} %copy-done, bf16[1,48,6,1,64,256]{5,4,1,2,3,0:T(8,128)(2,1)} %copy-done.1), kind=kLoop, calls=%fused_computation.12 | loop fusion | flops 9437184 | bytes 37748736 | tf_op jit(solution)/shard_map/stack | solution.py:76
  201.2 6.9 %gather_fusion.2 = bf16[6,2,64,256]{3,2,1,0:T(8,128)(2,1)S(1)} fusion(bf16[48,6,2,64,256]{4,3,0,1,2:T(8,128)(2,1)} %fusion.1, s32[6]{0:T(128)S(1)} %get-tuple-element.31), kind=kCustom, calls=%fused_computation.2 | custom fusion | bytes 786480 | tf_op jit(solution)/shard_map/gather | solution.py:93
  208.2 6.9 %gather_fusion.1 = bf16[6,2,64,256]{3,2,1,0:T(8,128)(2,1)S(1)} fusion(bf16[48,6,2,64,256]{4,3,0,1,2:T(8,128)(2,1)} %fusion.1, s32[6]{0:T(128)S(1)} %get-tuple-element.32), kind=kCustom, calls=%fused_computation.1 | custom fusion | bytes 786480 | tf_op jit(solution)/shard_map/gather | solution.py:93
  215.1 6.9 %gather_fusion = bf16[6,2,64,256]{3,2,1,0:T(8,128)(2,1)S(1)} fusion(bf16[48,6,2,64,256]{4,3,0,1,2:T(8,128)(2,1)} %fusion.1, s32[6]{0:T(128)S(1)} %get-tuple-element.33), kind=kCustom, calls=%fused_computation | custom fusion | bytes 786480 | tf_op jit(solution)/shard_map/gather | solution.py:93
  222.1 0.1 fusion.46
  222.2 0.1 fusion.47
  222.3 0.1 fusion.48
  222.4 0.1 fusion.32
  222.5 1.3 collective-permute-start
  223.8 4.6 collective-permute-start.1
  228.3 141.7 %all-to-all-done.1 = bf16[1,48,6,2,32,256]{5,4,2,3,0,1:T(8,128)(2,1)} async-done(((bf16[1,48,6,2,32,256]{5,4,2,3,0,1:T(8,128)(2,1)}), bf16[1,48,6,2,32,256]{5,4,2,3,0,1:T(8,128)(2,1)}, u32[]{:S(2)}, u32[]{:S(2)}) %all-to-all-start.1) | async-done | bytes 9437216 | tf_op jit(solution)/shard_map/all_to_all | solution.py:78
  370.0 9.1 %copy.78 = bf16[1,48,6,2,32,256]{5,4,3,2,1,0:T(8,128)(2,1)} copy(bf16[1,48,6,2,32,256]{5,4,2,3,0,1:T(8,128)(2,1)} %all-to-all-done.1) | data formatting | bytes 18874368 | tf_op jit(solution)/shard_map/all_to_all | solution.py:78
  379.1 9.5 %copy.79 = bf16[1,6,8,6,2,32,256]{6,5,4,3,2,1,0:T(8,128)(2,1)} copy(bf16[1,6,8,6,2,32,256]{6,5,4,3,1,2,0:T(8,128)(2,1)} %bitcast.186) | data formatting | bytes 18874368 | tf_op jit(solution)/shard_map/all_to_all | solution.py:78
  388.6 12.0 %fusion.14 = f32[6,2,256,2,256,1]{2,4,5,3,1,0:T(8,128)} fusion(bf16[6,48,2,32,256,1]{4,3,2,1,0,5:T(8,128)(2,1)} %bitcast.188, bf16[1,6,48,2,64,256]{5,4,3,2,1,0:T(8,128)(2,1)} %param.10), kind=kOutput, calls=%fused_computation.32 | convolution fusion | flops 4831838208 | bytes 25165824 | tf_op jit(solution)/shard_map/fijckr,fijeks->fcesir/dot_general | solution.py:79
  400.6 0.0 collective-permute-done
  400.6 0.0 collective-permute-done.1
  400.6 3.5 fusion.16
  404.2 2.2 fusion.64
  406.4 3.0 copy.83
  409.4 3.0 copy.84
  412.5 1.6 copy.85
  414.1 0.5 copy.86
  414.6 3.1 add_convert_fusion
  417.7 1.0 pad_maximum_fusion.1
  418.7 0.0 copy-start.2
  418.7 0.6 fusion.23
  419.4 0.1 multiply_convert_fusion.1
  419.5 0.7 maximum_bitcast_fusion.12
  420.2 0.0 all-reduce.2.cloned.1.call-update
  420.2 68.0 %all-reduce.2.cloned.1.call-done = bf16[1,2,2,128,128]{4,3,2,1,0:T(8,128)(2,1)} async-done(((bf16[1,2,2,128,128]{4,3,2,1,0:T(8,128)(2,1)}), bf16[1,2,2,128,128]{4,3,2,1,0:T(8,128)(2,1)}) %all-reduce.2.cloned.1.call-update) | async-done | bytes 131088 | tf_op jit(solution)/shard_map/psum | solution.py:132
  488.1 0.7 dynamic-slice_convert_fusion
  488.9 0.6 slice_bitcast_fusion.7
  489.5 0.0 copy-done.2
  (13 shorter events, 0.2 us)
Async XLA Ops:
  49.7 6.6 %copy-start.3 = (s32[1,48,6]{1,0,2:T(1,128)S(1)}, s32[1,48,6]{1,0,2:T(1,128)}, u32[]{:S(2)}) copy-start(s32[1,48,6]{1,0,2:T(1,128)} %param.9) | copy-start | bytes 3460
  52.1 24.3 %all-to-all-start = ((bf16[4,2,2,32,1536]{4,1,3,2,0:T(2,128)(2,1)}), bf16[4,2,2,32,1536]{4,1,3,2,0:T(2,128)(2,1)S(1)}, u32[]{:S(2)}, u32[]{:S(2)}) async-start(bf16[4,2,2,32,1536]{4,1,3,2,0:T(2,128)(2,1)} %copy.70), calls=%async_computation | async-start | bytes 3145728 | tf_op jit(solution)/shard_map/all_to_all | solution.py:65
  137.6 3.6 copy-start
  137.6 6.4 %copy-start.1 = (bf16[1,48,6,1,64,256]{5,4,1,2,3,0:T(8,128)(2,1)}, bf16[1,48,6,1,64,256]{5,4,1,2,3,0:T(8,128)(2,1)S(1)}, u32[]{:S(2)}) copy-start(bf16[1,48,6,1,64,256]{5,4,1,2,3,0:T(8,128)(2,1)S(1)} %get-tuple-element.5) | copy-start | bytes 28311556
  157.0 213.0 %all-to-all-start.1 = ((bf16[1,48,6,2,32,256]{5,4,2,3,0,1:T(8,128)(2,1)}), bf16[1,48,6,2,32,256]{5,4,2,3,0,1:T(8,128)(2,1)}, u32[]{:S(2)}, u32[]{:S(2)}) async-start(bf16[1,48,6,2,32,256]{5,4,2,3,0,1:T(8,128)(2,1)} %copy.77), calls=%async_computation.1 | async-start | bytes 18874368 | tf_op jit(solution)/shard_map/all_to_all | solution.py:78
  163.6 324.5 %all-reduce.2.cloned.1.call-start = ((), (), s32[]{:S(2)}) async-start(), calls=%async_computation.2 | async-start | bytes 262144 | tf_op jit(solution)/shard_map/psum | solution.py:132
  222.5 178.2 %collective-permute-start = (bf16[1,3,1,2,32,256]{5,4,3,2,1,0:T(8,128)(2,1)S(1)}, bf16[1,3,1,2,32,256]{5,4,3,2,1,0:T(8,128)(2,1)S(1)}, u32[]{:S(2)}, u32[]{:S(2)}) collective-permute-start(bf16[1,3,1,2,32,256]{5,4,3,2,1,0:T(8,128)(2,1)S(1)} %get-tuple-element.14), channel_id=1, source_target_pairs={{1,0},{2,1},{3,2},{4,3},{5,4},{6,5},{7,6},{9,8},{10,9},{11,10},{12... | collective-permute-start | bytes 294920 | tf_op jit(solution)/shard_map/ppermute | solution.py:19
  223.8 176.9 %collective-permute-start.1 = (bf16[1,3,1,2,32,256]{5,4,3,2,1,0:T(8,128)(2,1)S(1)}, bf16[1,3,1,2,32,256]{5,4,3,2,1,0:T(8,128)(2,1)S(1)}, u32[]{:S(2)}, u32[]{:S(2)}) collective-permute-start(bf16[1,3,1,2,32,256]{5,4,3,2,1,0:T(8,128)(2,1)S(1)} %get-tuple-element.15), channel_id=1, source_target_pairs={{0,1},{1,2},{2,3},{3,4},{4,5},{5,6},{6,7},{8,9},{9,10},{10,11},{11... | collective-permute-start | bytes 294920 | tf_op jit(solution)/shard_map/ppermute | solution.py:18
  418.7 70.7 %copy-start.2 = (bf16[1,2,128,1536]{3,2,1,0:T(8,128)(2,1)}, bf16[1,2,128,1536]{3,2,1,0:T(8,128)(2,1)S(1)}, u32[]{:S(2)}) copy-start(bf16[1,2,128,1536]{3,2,1,0:T(8,128)(2,1)S(1)} %get-tuple-element.12) | copy-start | bytes 2359300
Sparse Core Ops, SparseCore 0:
  420.3 67.7 all-reduce.1
where the time goes:
time: 498 us; the launch traced here: 496 us
  waiting for transfers between devices  230 us (46%)
  local copies, waits for them, and re-layouts  113 us (23%)
  other arithmetic  67 us (13%)
  matrix products  55.3 us (11%)
  starting transfers between devices  16.7 us (3%)
  between operations  14.3 us (3%)
    all_to_all x1, waiting for transfers between devices, on_device(): lax.all_to_all(lower_part, 'tile', split_axis=1, concat_axis=2, tiled=True)  142 us
    psum x1, waiting for transfers between devices, on_device(): lax.psum(gram_all.astype(jnp.bfloat16), 'tile').astype(jnp.float32)  68 us
    another operation x3, other arithmetic, on_device(): jnp.stack([coeff_real * rank_mask, coeff_imag * rank_mask], 3)  44.6 us
    dot_general x1, matrix products, on_device(): jnp.einsum('fijckr,fdsjr->fijcdks', v_factors, columns, preferred_element...  32.4 us
    gather x3, local copies, waits for them, and re-layouts, on_device(): u_band.append(u_factors[:, row_local, partner][:, :, :, half_depth:])  20.8 us
    gather x3, local copies, waits for them, and re-layouts, on_device(): picked = coeff_all[:, clipped, local_ids][:, :, :, half_depth:]  20.8 us
    all_to_all x1, waiting for transfers between devices, on_device(): lax.all_to_all(local_spec, 'freq', split_axis=0, concat_axis=3, tiled=True)  19.9 us
    broadcast_in_dim x2, local copies, waits for them, and re-layouts, gate_field(): kept = jnp.where(inside, shaped, jnp.zeros((), traces.dtype))  18.7 us
  transfers between devices with their start and end apart: 5, of which 3 were waited for; matrix products, arithmetic and copies ran while one was open for 18% of the time, Pallas kernels for 0%

commit v1 on v0

--- a/solution.py
+++ b/solution.py
@@ -129,7 +129,9 @@
     row_scale = jnp.where(row_ids < half_count, 1.0 / math.sqrt(R), 1.0 / R).astype(jnp.float32)
     gram_all = jnp.stack([gram_real * row_scale, gram_imag * row_scale], 1)
     gram_all = gram_all.reshape(f_local, 2, 2, half_count, half_count).transpose(0, 2, 1, 3, 4)
-    gram_total = lax.psum(gram_all.astype(jnp.bfloat16), "tile").astype(jnp.float32)
+    gram_total = jnp.sum(lax.all_gather(gram_all.astype(jnp.bfloat16), "tile"), axis=0).astype(
+        jnp.float32
+    )
     row_share = half_count // lax.axis_size("tile")
     own_rows = lax.dynamic_slice_in_dim(
         gram_total, lax.axis_index("tile") * row_share, row_share, 3

time: 498 us -> 468 us (0.940)
  waiting for transfers between devices: 230 us -> 199 us
    psum x1 -> x0, waiting for transfers between devices: 68 us -> none  [on_device(): lax.psum(gram_all.astype(jnp.bfloat16), 'tile').astype(jnp.float32)]
    all_gather x0 -> x1, waiting for transfers between devices: none -> 37.8 us  [on_device(): lax.all_gather(gram_all.astype(jnp.bfloat16), 'tile')]
  transfers between devices with their start and end apart: 5 -> 5, of which waited for: 3 -> 3; matrix products, arithmetic and copies ran while one was open for 18% -> 19% of each run, Pallas kernels for 0% -> 0%
where the time goes in v1:
time: 468 us; the launch traced here: 467 us
  waiting for transfers between devices  199 us (43%)
  local copies, waits for them, and re-layouts  113 us (24%)
  other arithmetic  67.7 us (14%)
  matrix products  55.3 us (12%)
  starting transfers between devices  16.7 us (4%)
  between operations  14.3 us (3%)
    all_to_all x1, waiting for transfers between devices, on_device(): lax.all_to_all(lower_part, 'tile', split_axis=1, concat_axis=2, tiled=True)  142 us
    another operation x3, other arithmetic, on_device(): jnp.stack([coeff_real * rank_mask, coeff_imag * rank_mask], 3)  44.6 us
    all_gather x1, waiting for transfers between devices, on_device(): lax.all_gather(gram_all.astype(jnp.bfloat16), 'tile')  37.8 us
    dot_general x1, matrix products, on_device(): jnp.einsum('fijckr,fdsjr->fijcdks', v_factors, columns, preferred_element...  32.4 us
    gather x3, local copies, waits for them, and re-layouts, on_device(): u_band.append(u_factors[:, row_local, partner][:, :, :, half_depth:])  20.8 us
    gather x3, local copies, waits for them, and re-layouts, on_device(): picked = coeff_all[:, clipped, local_ids][:, :, :, half_depth:]  20.8 us
    all_to_all x1, waiting for transfers between devices, on_device(): lax.all_to_all(local_spec, 'freq', split_axis=0, concat_axis=3, tiled=True)  19.9 us
    broadcast_in_dim x2, local copies, waits for them, and re-layouts, gate_field(): kept = jnp.where(inside, shaped, jnp.zeros((), traces.dtype))  18.7 us
  transfers between devices with their start and end apart: 5, of which 3 were waited for; matrix products, arithmetic and copies ran while one was open for 19% of the time, Pallas kernels for 0%

profile of v1, /device:TPU:0, one launch (start us, length us, event | category | flops | bytes accessed | tf_op | source)
XLA Modules:
  0.0 466.9 jit_solution(6777723791822644184)
XLA Ops:
  7.2 0.7 broadcast_add_fusion
  7.9 0.8 copy.63
  8.6 0.1 multiply_convert_fusion.2
  8.7 0.1 copy.64
  8.8 0.1 fusion.50
  8.9 4.3 broadcast_in_dim.81
  13.2 14.4 %copy.65 = pred[32,128,1536]{2,1,0:T(8,128)(4,1)} copy(pred[32,128,1536]{1,2,0:T(8,128)(4,1)} %bitcast.189) | data formatting | bytes 12582912 | tf_op jit(solution)/shard_map/jit(_where)/broadcast_in_dim | solution.py:47
  27.6 15.3 %select_bitcast_fusion.1 = (bf16[1,32,128,1536]{3,2,1,0:T(8,128)(2,1)S(1)}, bf16[1,32,128,1536]{3,2,1,0:T(8,128)(2,1)}) fusion(pred[32,128,1536]{2,1,0:T(8,128)(4,1)} %copy.65, bf16[32,128,1536]{2,1,0:T(8,128)(2,1)} %param.6, bf16[32,128,1536]{2,1,0:T(8,128)(2,1)} %param.7), kind=kLoop, calls=%fused_computation.27 | loop fusion | flops 12582912 | bytes 56623104 | tf_op jit(solution)/shard_map/jit(_where)/select_n | solution.py:47
  42.9 6.8 %fusion.18 = bf16[4,2,2,32,1536]{4,0,1,3,2:T(4,128)(2,1)S(1)} fusion(bf16[1,32,128,1536]{3,2,1,0:T(8,128)(2,1)} %get-tuple-element.11, bf16[1,32,128,1536]{3,2,1,0:T(8,128)(2,1)S(1)} %get-tuple-element.10, bf16[1,4,128]{2,1,0:T(4,128)(2,1)S(1)} %get-tuple-element.24, bf16[1,4,128]{2,1,0:T(4,128)(2,1)S(1)} %get-tuple-element.25), kind=kOutput, calls=%fused_computation.37 | convolution fusion | flops 252448768 | bytes 26740736 | tf_op jit(solution)/shard_map/cft,qstr->fcqsr/dot_general | solution.py:62
  49.7 0.0 copy-start.3
  49.8 2.4 copy.67
  52.1 4.2 all-to-all-start
  56.4 0.0 copy-done.3
  56.4 0.1 fusion.49
  56.5 19.9 %all-to-all-done = bf16[4,2,2,32,1536]{4,1,3,2,0:T(2,128)(2,1)S(1)} async-done(((bf16[4,2,2,32,1536]{4,1,3,2,0:T(2,128)(2,1)}), bf16[4,2,2,32,1536]{4,1,3,2,0:T(2,128)(2,1)S(1)}, u32[]{:S(2)}, u32[]{:S(2)}) %all-to-all-start) | async-done | bytes 1572896 | tf_op jit(solution)/shard_map/all_to_all | solution.py:65
  76.4 1.4 copy.68
  77.8 3.3 reshape.609
  81.1 32.4 %convolution_bitcast_fusion = f32[1,48,6,2,2,64,256]{6,5,3,1,4,2,0:T(8,128)} fusion(bf16[2,256,6,256,1,1]{3,2,1,0,5,4:T(8,128)(2,1)S(1)} %bitcast.191, bf16[1,48,6,2,64,256]{5,4,3,2,1,0:T(8,128)(2,1)} %param.11), kind=kOutput, calls=%fused_computation.6 | convolution fusion | flops 9663676416 | bytes 95944704 | tf_op jit(solution)/shard_map/fijckr,fdsjr->fijcdks/dot_general | solution.py:69
  113.5 24.0 %fusion.12 = (bf16[1,48,6,1,64,256]{5,4,1,2,3,0:T(8,128)(2,1)S(1)}, bf16[1,48,6,1,64,256]{5,4,1,2,3,0:T(8,128)(2,1)S(1)}) fusion(f32[1,48,6,2,2,64,256]{6,5,3,1,4,2,0:T(8,128)} %convolution_bitcast_fusion, f32[48,6,64]{2,0,1:T(8,128)S(1)} %fusion.49, f32[256]{0:T(256)S(1)} %compare_select_fusion.4), kind=kLoop, calls=%fused_computation.29 | loop fusion | flops 37748736 | bytes 94446592 | tf_op jit(solution)/shard_map/stack | solution.py:76
  137.6 0.0 copy-start
  137.6 0.0 copy-start.1
  137.6 3.6 copy-done
  141.2 2.7 copy-done.1
  143.9 4.1 fusion.13
  148.0 9.0 %copy.74 = bf16[1,48,6,2,32,256]{5,4,2,3,0,1:T(8,128)(2,1)} copy(bf16[1,48,6,2,32,256]{5,4,1,2,3,0:T(8,128)(2,1)} %fusion.13) | data formatting | bytes 18874368 | tf_op jit(solution)/shard_map/slice | solution.py:77
  157.0 6.6 %all-to-all-start.1 = ((bf16[1,48,6,2,32,256]{5,4,2,3,0,1:T(8,128)(2,1)}), bf16[1,48,6,2,32,256]{5,4,2,3,0,1:T(8,128)(2,1)}, u32[]{:S(2)}, u32[]{:S(2)}) async-start(bf16[1,48,6,2,32,256]{5,4,2,3,0,1:T(8,128)(2,1)} %copy.74), calls=%async_computation.1 | async-start | bytes 18874368 | tf_op jit(solution)/shard_map/all_to_all | solution.py:78
  163.6 0.0 all-gather.3.cloned.1.call-start
  163.7 6.9 %gather_fusion.5 = bf16[6,2,64,256]{3,2,1,0:T(8,128)(2,1)S(1)} fusion(bf16[6,48,2,64,256]{4,3,2,1,0:T(8,128)(2,1)} %bitcast.207, s32[6]{0:T(128)S(1)} %get-tuple-element.28), kind=kCustom, calls=%fused_computation.5 | custom fusion | bytes 786480 | tf_op jit(solution)/shard_map/gather | solution.py:108
  170.7 6.9 %gather_fusion.4 = bf16[6,2,64,256]{3,2,1,0:T(8,128)(2,1)S(1)} fusion(bf16[6,48,2,64,256]{4,3,2,1,0:T(8,128)(2,1)} %bitcast.208, s32[6]{0:T(128)S(1)} %get-tuple-element.29), kind=kCustom, calls=%fused_computation.4 | custom fusion | bytes 786480 | tf_op jit(solution)/shard_map/gather | solution.py:108
  177.6 6.9 %gather_fusion.3 = bf16[6,2,64,256]{3,2,1,0:T(8,128)(2,1)S(1)} fusion(bf16[6,48,2,64,256]{4,3,2,1,0:T(8,128)(2,1)} %bitcast.209, s32[6]{0:T(128)S(1)} %get-tuple-element.30), kind=kCustom, calls=%fused_computation.3 | custom fusion | bytes 786480 | tf_op jit(solution)/shard_map/gather | solution.py:108
  184.7 16.5 %fusion.1 = bf16[48,6,2,64,256]{4,3,0,1,2:T(8,128)(2,1)} fusion(bf16[1,48,6,1,64,256]{5,4,1,2,3,0:T(8,128)(2,1)} %copy-done, bf16[1,48,6,1,64,256]{5,4,1,2,3,0:T(8,128)(2,1)} %copy-done.1), kind=kLoop, calls=%fused_computation.12 | loop fusion | flops 9437184 | bytes 37748736 | tf_op jit(solution)/shard_map/stack | solution.py:76
  201.2 6.9 %gather_fusion.2 = bf16[6,2,64,256]{3,2,1,0:T(8,128)(2,1)S(1)} fusion(bf16[48,6,2,64,256]{4,3,0,1,2:T(8,128)(2,1)} %fusion.1, s32[6]{0:T(128)S(1)} %get-tuple-element.31), kind=kCustom, calls=%fused_computation.2 | custom fusion | bytes 786480 | tf_op jit(solution)/shard_map/gather | solution.py:93
  208.2 6.9 %gather_fusion.1 = bf16[6,2,64,256]{3,2,1,0:T(8,128)(2,1)S(1)} fusion(bf16[48,6,2,64,256]{4,3,0,1,2:T(8,128)(2,1)} %fusion.1, s32[6]{0:T(128)S(1)} %get-tuple-element.32), kind=kCustom, calls=%fused_computation.1 | custom fusion | bytes 786480 | tf_op jit(solution)/shard_map/gather | solution.py:93
  215.1 6.9 %gather_fusion = bf16[6,2,64,256]{3,2,1,0:T(8,128)(2,1)S(1)} fusion(bf16[48,6,2,64,256]{4,3,0,1,2:T(8,128)(2,1)} %fusion.1, s32[6]{0:T(128)S(1)} %get-tuple-element.33), kind=kCustom, calls=%fused_computation | custom fusion | bytes 786480 | tf_op jit(solution)/shard_map/gather | solution.py:93
  222.1 0.1 fusion.46
  222.2 0.1 fusion.47
  222.3 0.1 fusion.48
  222.4 0.1 fusion.32
  222.5 1.3 collective-permute-start
  223.8 4.6 collective-permute-start.1
  228.3 141.7 %all-to-all-done.1 = bf16[1,48,6,2,32,256]{5,4,2,3,0,1:T(8,128)(2,1)} async-done(((bf16[1,48,6,2,32,256]{5,4,2,3,0,1:T(8,128)(2,1)}), bf16[1,48,6,2,32,256]{5,4,2,3,0,1:T(8,128)(2,1)}, u32[]{:S(2)}, u32[]{:S(2)}) %all-to-all-start.1) | async-done | bytes 9437216 | tf_op jit(solution)/shard_map/all_to_all | solution.py:78
  370.0 9.1 %copy.75 = bf16[1,48,6,2,32,256]{5,4,3,2,1,0:T(8,128)(2,1)} copy(bf16[1,48,6,2,32,256]{5,4,2,3,0,1:T(8,128)(2,1)} %all-to-all-done.1) | data formatting | bytes 18874368 | tf_op jit(solution)/shard_map/all_to_all | solution.py:78
  379.1 9.5 %copy.76 = bf16[1,6,8,6,2,32,256]{6,5,4,3,2,1,0:T(8,128)(2,1)} copy(bf16[1,6,8,6,2,32,256]{6,5,4,3,1,2,0:T(8,128)(2,1)} %bitcast.188) | data formatting | bytes 18874368 | tf_op jit(solution)/shard_map/all_to_all | solution.py:78
  388.6 12.0 %fusion.14 = f32[6,2,256,2,256,1]{2,4,5,3,1,0:T(8,128)} fusion(bf16[6,48,2,32,256,1]{4,3,2,1,0,5:T(8,128)(2,1)} %bitcast.190, bf16[1,6,48,2,64,256]{5,4,3,2,1,0:T(8,128)(2,1)} %param.10), kind=kOutput, calls=%fused_computation.32 | convolution fusion | flops 4831838208 | bytes 25165824 | tf_op jit(solution)/shard_map/fijckr,fijeks->fcesir/dot_general | solution.py:79
  400.6 0.0 collective-permute-done
  400.6 0.0 collective-permute-done.1
  400.6 3.5 fusion.16
  404.2 2.2 fusion.64
  406.4 3.0 copy.80
  409.4 3.0 copy.81
  412.5 1.6 copy.82
  414.1 0.5 copy.83
  414.6 3.1 add_convert_fusion
  417.7 1.0 pad_maximum_fusion.1
  418.7 0.0 copy-start.2
  418.7 0.6 fusion.23
  419.4 0.1 multiply_convert_fusion.1
  419.5 0.7 maximum_bitcast_fusion.12
  420.2 0.0 all-gather.3.cloned.1.call-update
  420.2 37.8 %all-gather.3.cloned.1.call-done = bf16[8,2,2,128,128]{4,3,2,1,0:T(8,128)(2,1)} async-done(((bf16[1,2,2,128,128]{4,3,2,1,0:T(8,128)(2,1)}), bf16[8,2,2,128,128]{4,3,2,1,0:T(8,128)(2,1)}) %all-gather.3.cloned.1.call-update) | async-done | bytes 1048592 | tf_op jit(solution)/shard_map/all_gather | solution.py:132
  458.0 1.4 reduce.2
  459.4 0.6 slice_bitcast_fusion.7
  460.1 0.0 copy-done.2
  (14 shorter events, 0.2 us)
Async XLA Ops:
  49.7 6.6 %copy-start.3 = (s32[1,48,6]{1,0,2:T(1,128)S(1)}, s32[1,48,6]{1,0,2:T(1,128)}, u32[]{:S(2)}) copy-start(s32[1,48,6]{1,0,2:T(1,128)} %param.9) | copy-start | bytes 3460
  52.1 24.3 %all-to-all-start = ((bf16[4,2,2,32,1536]{4,1,3,2,0:T(2,128)(2,1)}), bf16[4,2,2,32,1536]{4,1,3,2,0:T(2,128)(2,1)S(1)}, u32[]{:S(2)}, u32[]{:S(2)}) async-start(bf16[4,2,2,32,1536]{4,1,3,2,0:T(2,128)(2,1)} %copy.67), calls=%async_computation | async-start | bytes 3145728 | tf_op jit(solution)/shard_map/all_to_all | solution.py:65
  137.6 3.6 copy-start
  137.6 6.4 %copy-start.1 = (bf16[1,48,6,1,64,256]{5,4,1,2,3,0:T(8,128)(2,1)}, bf16[1,48,6,1,64,256]{5,4,1,2,3,0:T(8,128)(2,1)S(1)}, u32[]{:S(2)}) copy-start(bf16[1,48,6,1,64,256]{5,4,1,2,3,0:T(8,128)(2,1)S(1)} %get-tuple-element.5) | copy-start | bytes 28311556
  157.0 213.0 %all-to-all-start.1 = ((bf16[1,48,6,2,32,256]{5,4,2,3,0,1:T(8,128)(2,1)}), bf16[1,48,6,2,32,256]{5,4,2,3,0,1:T(8,128)(2,1)}, u32[]{:S(2)}, u32[]{:S(2)}) async-start(bf16[1,48,6,2,32,256]{5,4,2,3,0,1:T(8,128)(2,1)} %copy.74), calls=%async_computation.1 | async-start | bytes 18874368 | tf_op jit(solution)/shard_map/all_to_all | solution.py:78
  163.6 294.4 %all-gather.3.cloned.1.call-start = ((), (), s32[]{:S(2)}) async-start(), calls=%async_computation.2 | async-start | bytes 1179648 | tf_op jit(solution)/shard_map/all_gather | solution.py:132
  222.5 178.2 %collective-permute-start = (bf16[1,3,1,2,32,256]{5,4,3,2,1,0:T(8,128)(2,1)S(1)}, bf16[1,3,1,2,32,256]{5,4,3,2,1,0:T(8,128)(2,1)S(1)}, u32[]{:S(2)}, u32[]{:S(2)}) collective-permute-start(bf16[1,3,1,2,32,256]{5,4,3,2,1,0:T(8,128)(2,1)S(1)} %get-tuple-element.14), channel_id=1, source_target_pairs={{1,0},{2,1},{3,2},{4,3},{5,4},{6,5},{7,6},{9,8},{10,9},{11,10},{12... | collective-permute-start | bytes 294920 | tf_op jit(solution)/shard_map/ppermute | solution.py:19
  223.8 176.9 %collective-permute-start.1 = (bf16[1,3,1,2,32,256]{5,4,3,2,1,0:T(8,128)(2,1)S(1)}, bf16[1,3,1,2,32,256]{5,4,3,2,1,0:T(8,128)(2,1)S(1)}, u32[]{:S(2)}, u32[]{:S(2)}) collective-permute-start(bf16[1,3,1,2,32,256]{5,4,3,2,1,0:T(8,128)(2,1)S(1)} %get-tuple-element.15), channel_id=1, source_target_pairs={{0,1},{1,2},{2,3},{3,4},{4,5},{5,6},{6,7},{8,9},{9,10},{10,11},{11... | collective-permute-start | bytes 294920 | tf_op jit(solution)/shard_map/ppermute | solution.py:18
  418.7 41.3 %copy-start.2 = (bf16[1,2,128,1536]{3,2,1,0:T(8,128)(2,1)}, bf16[1,2,128,1536]{3,2,1,0:T(8,128)(2,1)S(1)}, u32[]{:S(2)}) copy-start(bf16[1,2,128,1536]{3,2,1,0:T(8,128)(2,1)S(1)} %get-tuple-element.12) | copy-start | bytes 2359300
Sparse Core Ops, SparseCore 0:
  420.3 37.6 all-gather.2
